TPU v7x, 32 devices: a whole 2x2x4 slice. The times are simulated.
32 devices in a mesh: gx: 4 (over x, core), gy: 8 (over z, y).
Axes of the slice: x: 2, y: 2, z: 4, core: 2. Of those that a mesh axis runs over, the one named last changes fastest.
Arguments:
- patches: bfloat16 [4096, 1664], P('gy', 'gx'), may hold values from -6 to 6
- segment_ids: int32 [4096], P('gy'), may hold values from 0 to 31, as said below
- image_requests: int32 [32], replicated, may hold values from 0 to 7
- merge_index: int32 [1024, 4], P('gy'), may hold values from 0 to 4095, as said below
- qkv_weight: bfloat16 [1664, 3, 1664], P('gy', None, 'gx'), may hold values from -128 to 128
- out_weight: bfloat16 [1664, 1664], P('gx', 'gy'), may hold values from -0.15625 to 0.15625
- up_weight: bfloat16 [1664, 8192], P('gy', 'gx'), may hold values from -0.15625 to 0.15625
- down_weight: bfloat16 [8192, 1664], P('gx', 'gy'), may hold values from -0.0625 to 0.0625
- merge_weight: bfloat16 [6656, 4096], P('gy', 'gx'), may hold values from -0.078125 to 0.078125
Outputs:
- merged: bfloat16 [1024, 4096], P('gy', 'gx')
- request_norms: float32 [8], replicated
- top_logit: float32 [], replicated
Inputs may be any that keep to these rules, and one draw needn't show every extreme that they name: `segment_ids`: segment ids never fall along the tokens; the 512 tokens of block b (tokens b * 512 onward) hold exactly the images b * 4 to (b + 1) * 4 - 1, each a multiple of 4 tokens long. `merge_index`: every token stands in exactly one merged row; the four tokens of merged row m belong to one image, in the block of 512 tokens that holds token 4 * m.
All inputs are finite; a program needn't handle non-finite values.
Results may differ from a plain program's by a relative error of at most 0.011.
Values may be sent and summed in bfloat16 or wider, within the bound.
A program may use at most 128 MiB of HBM per device.

v0:
```python
import math
import jax
import jax.numpy as jnp
from jax import lax
from jax.sharding import PartitionSpec as P

HEAD = 104
IMG_GRP = 4


def layer_norm(values):
    center = jnp.mean(values, axis=-1, keepdims=True)
    square = jnp.mean(values * values, axis=-1, keepdims=True)
    return (values - center) * lax.rsqrt(square - center * center + 1e-06)


def add_columns(left, piece):
    flat = piece.reshape(piece.shape[0], -1)
    return jnp.dot(left, flat, preferred_element_type=jnp.float32)


def finish_sum(head_partial, stream_full, feat_share):
    own_index = lax.axis_index("gx")
    summed = lax.psum(head_partial, "gx")
    new_full = (stream_full.astype(jnp.float32) + summed).astype(jnp.bfloat16)
    new_share = lax.dynamic_slice_in_dim(new_full, own_index * feat_share, feat_share, 1)
    return (new_full, new_share)


def per_device(
    patches,
    segment_ids,
    image_requests,
    merge_index,
    qkv_weight,
    out_weight,
    up_weight,
    down_weight,
    merge_weight,
):
    tok_rows = patches.shape[0]
    feat_share = patches.shape[1]
    group_index = lax.axis_index("gy")
    stream_full = lax.all_gather(patches, "gx", axis=1, tiled=True)
    normed = layer_norm(stream_full.astype(jnp.float32)).astype(jnp.bfloat16)
    head_share = qkv_weight.shape[2]
    local_heads = head_share // HEAD
    projected = add_columns(normed, lax.all_gather(qkv_weight, "gy", axis=0, tiled=True))
    projected = projected.astype(jnp.bfloat16).reshape(tok_rows, 3, local_heads, HEAD)
    scores = jnp.einsum(
        "qhe,khe->hqk", projected[:, 0], projected[:, 1], preferred_element_type=jnp.float32
    ) / math.sqrt(HEAD)
    allowed = segment_ids[:, None] == segment_ids[None, :]
    scores = jnp.where(allowed[None], scores, -1e30)
    probs = jax.nn.softmax(scores, axis=-1).astype(jnp.bfloat16)
    mixed = jnp.einsum("hqk,khe->qhe", probs, projected[:, 2], preferred_element_type=jnp.float32)
    mixed = mixed.astype(jnp.bfloat16).reshape(tok_rows, head_share)
    head_partial = jnp.dot(
        mixed,
        lax.all_gather(out_weight, "gy", axis=1, tiled=True),
        preferred_element_type=jnp.float32,
    )
    stream_full, stream_share = finish_sum(head_partial, stream_full, feat_share)
    normed_two = layer_norm(stream_full.astype(jnp.float32)).astype(jnp.bfloat16)
    hidden = add_columns(normed_two, lax.all_gather(up_weight, "gy", axis=0, tiled=True))
    hidden = jax.nn.gelu(hidden, approximate=False).astype(jnp.bfloat16)
    unit_partial = jnp.dot(
        hidden,
        lax.all_gather(down_weight, "gy", axis=1, tiled=True),
        preferred_element_type=jnp.float32,
    )
    final_full, final_share = finish_sum(unit_partial, stream_full, feat_share)
    row_squares = jnp.sum(jnp.square(final_share.astype(jnp.float32)), axis=1)
    image_ids = group_index * IMG_GRP + jnp.arange(IMG_GRP, dtype=jnp.int32)
    member = segment_ids[:, None] == image_ids[None, :]
    image_sq = jnp.sum(jnp.where(member, row_squares[:, None], 0.0), axis=0)
    local_requests = lax.dynamic_slice_in_dim(image_requests, group_index * IMG_GRP, IMG_GRP)
    request_count = image_requests.shape[0] // 4
    owner = local_requests[:, None] == jnp.arange(request_count, dtype=jnp.int32)[None, :]
    request_part = jnp.sum(jnp.where(owner, image_sq[:, None], 0.0), axis=0)
    local_index = (merge_index - group_index * tok_rows).reshape(-1)
    joined = jnp.take(final_full, local_index, axis=0).reshape(
        merge_index.shape[0], 4 * final_full.shape[1]
    )
    logits = add_columns(joined, lax.all_gather(merge_weight, "gy", axis=0, tiled=True))
    local_top = jnp.max(logits)
    request_sq = lax.psum(request_part, ("gx", "gy"))
    top_logit = lax.pmax(local_top, ("gx", "gy"))
    return (logits.astype(jnp.bfloat16), jnp.sqrt(request_sq), top_logit)


def solution(mesh):
    in_specs = (
        P("gy", "gx"),
        P("gy"),
        P(),
        P("gy", None),
        P("gy", None, "gx"),
        P("gx", "gy"),
        P("gy", "gx"),
        P("gx", "gy"),
        P("gy", "gx"),
    )
    out_specs = (P("gy", "gx"), P(), P())
    return jax.shard_map(
        per_device, mesh=mesh, in_specs=in_specs, out_specs=out_specs, check_vma=False
    )
```

profile of v0, /device:TPU:0, one launch (start us, length us, event | category | flops | bytes accessed | tf_op | source)
XLA Modules:
  0.0 815.3 jit_solution(6109742581719975203)
XLA Ops:
  7.9 2.6 copy.29
  10.6 1.7 copy.32
  13.4 19.3 %all-gather.7.cloned.1.call-done = bf16[512,1664]{0,1:T(8,128)(2,1)} async-done(((bf16[512,416]{0,1:T(8,128)(2,1)}), bf16[512,1664]{0,1:T(8,128)(2,1)}) %all-gather.7.cloned.1.call-update) | async-done | bytes 1703952 | tf_op jit(solution)/shard_map/all_gather | solution.py:44
  32.7 2.7 copy.28
  36.1 104.4 %all-gather.9.cloned.1.call-done = bf16[1664,3,416]{2,1,0:T(4,128)(2,1)} async-done(((bf16[208,3,416]{2,1,0:T(4,128)(2,1)}), bf16[1664,3,416]{2,1,0:T(4,128)(2,1)}) %all-gather.9.cloned.1.call-update) | async-done | bytes 4153360 | tf_op jit(solution)/shard_map/all_gather | solution.py:48
  140.5 11.3 %copy.30 = bf16[1664,3,416]{0,2,1:T(8,128)(2,1)} copy(bf16[1664,3,416]{2,1,0:T(4,128)(2,1)} %all-gather.9.cloned.1.call-done) | data formatting | bytes 8306688 | tf_op jit(solution)/shard_map/all_gather | solution.py:48
  151.7 4.8 convolution_convert_fusion
  157.3 2.1 fusion.109
  160.0 26.7 %all-gather.11.cloned.1.call-done = bf16[416,1664]{0,1:T(8,128)(2,1)} async-done(((bf16[416,208]{0,1:T(8,128)(2,1)}), bf16[416,1664]{0,1:T(8,128)(2,1)}) %all-gather.11.cloned.1.call-update) | async-done | bytes 1384464 | tf_op jit(solution)/shard_map/all_gather | solution.py:60
  186.7 4.4 fusion.110
  192.5 70.4 %all-reduce.3.cloned.1.call-done = f32[512,1664]{1,0:T(8,128)} async-done(((f32[512,1664]{1,0:T(8,128)}), f32[512,1664]{1,0:T(8,128)}) %all-reduce.3.cloned.1.call-update) | async-done | bytes 3407888 | tf_op jit(solution)/shard_map/psum | solution.py:24
  262.9 2.7 convert_reduce_fusion
  265.6 105.1 %all-gather.13.cloned.1.call-done = bf16[1664,2048]{1,0:T(8,128)(2,1)} async-done(((bf16[208,2048]{1,0:T(8,128)(2,1)}), bf16[1664,2048]{1,0:T(8,128)(2,1)}) %all-gather.13.cloned.1.call-update) | async-done | bytes 6815760 | tf_op jit(solution)/shard_map/all_gather | solution.py:65
  370.6 105.8 %all-gather.15.cloned.1.call-done = bf16[2048,1664]{0,1:T(8,128)(2,1)} async-done(((bf16[2048,208]{0,1:T(8,128)(2,1)}), bf16[2048,1664]{0,1:T(8,128)(2,1)}) %all-gather.15.cloned.1.call-update) | async-done | bytes 6815760 | tf_op jit(solution)/shard_map/all_gather | solution.py:69
  476.5 21.5 %fusion.20 = f32[512,1664]{1,0:T(8,128)} fusion(bf16[2048,1664]{0,1:T(8,128)(2,1)} %all-gather.15.cloned.1.call-done, bf16[1664,2048]{1,0:T(8,128)(2,1)} %all-gather.13.cloned.1.call-done, bf16[512,1664]{1,0:T(8,128)(2,1)S(1)} %get-tuple-element.7, f32[512]{0:T(512)S(1)} %get-tuple-element.13, f32[512]{0:T(512)S(1)} %get-tuple-element.12), kind=kOutput, calls=%fused_computation.42 | convolution fusion | flops 7050887168 | bytes 18747392 | tf_op jit(solution)/shard_map/dot_general | solution.py:67
  499.2 69.8 %all-reduce.5.cloned.1.call-done = f32[512,1664]{1,0:T(8,128)} async-done(((f32[512,1664]{1,0:T(8,128)}), f32[512,1664]{1,0:T(8,128)}) %all-reduce.5.cloned.1.call-update) | async-done | bytes 3407888 | tf_op jit(solution)/shard_map/psum | solution.py:24
  569.0 2.2 fusion.18
  572.4 1.3 copy.35
  573.8 42.4 %psum.23 = f32[8]{0:T(128)S(1)} all-reduce(f32[8]{0:T(128)S(1)} %select_reduce_fusion.1), channel_id=1, replica_groups=mesh['gx'=4,'gy'=8] {'gx','gy'}, use_global_device_ids=true, to_apply=%region_11.12 | all-reduce | flops 8 | bytes 64 | tf_op jit(solution)/shard_map/psum | solution.py:87
  616.2 2.3 gather_fusion
  618.5 1.2 gather.7
  620.2 141.2 %all-gather.17.cloned.1.call-done = bf16[6656,1024]{1,0:T(8,128)(2,1)} async-done(((bf16[832,1024]{1,0:T(8,128)(2,1)}), bf16[6656,1024]{1,0:T(8,128)(2,1)}) %all-gather.17.cloned.1.call-update) | async-done | bytes 13631504 | tf_op jit(solution)/shard_map/all_gather | solution.py:85
  761.5 8.4 %fusion.108 = (f32[]{:T(128)}, bf16[128,1024]{1,0:T(8,128)(2,1)}) fusion(bf16[6656,1024]{1,0:T(8,128)(2,1)} %all-gather.17.cloned.1.call-done, pred[128,6656]{1,0:T(8,128)(4,1)} %bitcast.26, bf16[128,6656]{1,0:T(8,128)(2,1)S(1)} %gather.7), kind=kOutput, calls=%fused_computation.138 | convolution fusion | flops 1745944576 | bytes 16449540 | tf_op jit(solution)/shard_map/dot_general | solution.py:19
  769.9 38.6 %pmax.7 = f32[]{:T(128)} all-reduce(f32[]{:T(128)} %get-tuple-element.10), channel_id=1, replica_groups=mesh['gx'=4,'gy'=8] {'gx','gy'}, use_global_device_ids=true, to_apply=%region_13.14 | all-reduce | flops 1 | bytes 8 | tf_op jit(solution)/shard_map/pmax | solution.py:88
  (41 shorter events, 8.0 us)
Async XLA Ops:
  7.2 25.5 %all-gather.7.cloned.1.call-start = ((), (), s32[]{:S(2)}) async-start(), calls=%async_computation | async-start | bytes 2129920 | tf_op jit(solution)/shard_map/all_gather | solution.py:44
  7.9 132.6 %all-gather.9.cloned.1.call-start = ((), (), s32[]{:S(2)}) async-start(), calls=%async_computation.1 | async-start | bytes 7667712 | tf_op jit(solution)/shard_map/all_gather | solution.py:48
  10.6 176.1 %all-gather.11.cloned.1.call-start = ((), (), s32[]{:S(2)}) async-start(), calls=%async_computation.2 | async-start | bytes 1916928 | tf_op jit(solution)/shard_map/all_gather | solution.py:60
  12.4 250.5 %all-reduce.3.cloned.1.call-start = ((), (), s32[]{:S(2)}) async-start(), calls=%async_computation.3 | async-start | bytes 6815744 | tf_op jit(solution)/shard_map/psum | solution.py:24
  191.1 179.6 %all-gather.13.cloned.1.call-start = ((), (), s32[]{:S(2)}) async-start(), calls=%async_computation.4 | async-start | bytes 7667712 | tf_op jit(solution)/shard_map/all_gather | solution.py:65
  191.7 284.8 %all-gather.15.cloned.1.call-start = ((), (), s32[]{:S(2)}) async-start(), calls=%async_computation.5 | async-start | bytes 7667712 | tf_op jit(solution)/shard_map/all_gather | solution.py:69
  192.3 376.7 %all-reduce.5.cloned.1.call-start = ((), (), s32[]{:S(2)}) async-start(), calls=%async_computation.6 | async-start | bytes 6815744 | tf_op jit(solution)/shard_map/psum | solution.py:24
  497.9 0.8 copy-start.1
  497.9 1.2 copy-start.2
  498.0 263.5 %all-gather.17.cloned.1.call-start = ((), (), s32[]{:S(2)}) async-start(), calls=%async_computation.7 | async-start | bytes 15335424 | tf_op jit(solution)/shard_map/all_gather | solution.py:85
  498.7 72.9 %copy-start = (s32[512]{0:T(512)S(1)}, s32[512]{0:T(512)}, u32[]{:S(2)}) copy-start(s32[512]{0:T(512)} %param.10) | copy-start | bytes 6148
Sparse Core Ops, SparseCore 0:
  9.6 23.0 all-gather.6
  34.9 105.5 all-gather.8
  143.2 43.4 all-gather.10
  191.2 71.6 all-reduce.2
  264.9 105.6 all-gather.12
  372.7 103.7 all-gather.14
  498.1 70.8 all-reduce.4
  571.2 190.2 all-gather.16
where the time goes:
time: 816 us; the launch traced here: 815 us
  waiting for transfers between devices  645 us (79%)
  blocking collectives  81.1 us (10%)
  matrix products  40.3 us (5%)
  local copies, waits for them, and re-layouts  24.7 us (3%)
  between operations  14.3 us (2%)
  other arithmetic  9.36 us (1%)
    all_gather x1, waiting for transfers between devices, per_device(): lax.all_gather(merge_weight, 'gy', axis=0, tiled=True)  141 us
    psum x2, waiting for transfers between devices, finish_sum(): summed = lax.psum(head_partial, 'gx')  140 us
    all_gather x1, waiting for transfers between devices, per_device(): lax.all_gather(down_weight, 'gy', axis=1, tiled=True)  106 us
    all_gather x1, waiting for transfers between devices, per_device(): lax.all_gather(up_weight, 'gy', axis=0, tiled=True)  105 us
    all_gather x1, waiting for transfers between devices, per_device(): lax.all_gather(qkv_weight, 'gy', axis=0, tiled=True)  104 us
    psum x1, blocking collectives, per_device(): request_sq = lax.psum(request_part, ('gx', 'gy'))  42.4 us
    pmax x1, blocking collectives, per_device(): top_logit = lax.pmax(local_top, ('gx', 'gy'))  38.6 us
    all_gather x1, waiting for transfers between devices, per_device(): lax.all_gather(out_weight, 'gy', axis=1, tiled=True)  26.7 us
  transfers between devices with their start and end apart: 8, of which 8 were waited for; matrix products, arithmetic and copies ran while one was open for 5% of the time, Pallas kernels for 0%

commit v1 on v0

--- a/solution.py
+++ b/solution.py
@@ -1,3 +1,4 @@
+import functools
 import math
 import jax
 import jax.numpy as jnp
@@ -6,6 +7,20 @@
 
 HEAD = 104
 IMG_GRP = 4
+
+
+def convert_lots_all(a0, axis_k):
+    workers = lax.axis_size("gy")
+    views = [a0]
+    for i in range(1, workers):
+        views.append(
+            lax.ppermute(views[i - 1], "gy", [(h, (h - 1) % workers) for h in range(workers)])
+        )
+    mat_out = jnp.concatenate(views, axis=axis_k)
+    return jnp.roll(mat_out, lax.axis_index("gy") * a0.shape[axis_k], axis_k)
+
+
+recast_the_surface = functools.partial(convert_lots_all, axis_k=1)
 
 
 def layer_norm(values):
@@ -65,9 +80,7 @@
     hidden = add_columns(normed_two, lax.all_gather(up_weight, "gy", axis=0, tiled=True))
     hidden = jax.nn.gelu(hidden, approximate=False).astype(jnp.bfloat16)
     unit_partial = jnp.dot(
-        hidden,
-        lax.all_gather(down_weight, "gy", axis=1, tiled=True),
-        preferred_element_type=jnp.float32,
+        hidden, recast_the_surface(down_weight), preferred_element_type=jnp.float32
     )
     final_full, final_share = finish_sum(unit_partial, stream_full, feat_share)
     row_squares = jnp.sum(jnp.square(final_share.astype(jnp.float32)), axis=1)

time: 816 us -> 763 us (0.935)
  waiting for transfers between devices: 645 us -> 533 us
  starting transfers between devices: 0.5 us -> 33.9 us
  local copies, waits for them, and re-layouts: 24.7 us -> 49.2 us
    ppermute x0 -> x7, waiting for transfers between devices: none -> 131 us  [convert_lots_all(): lax.ppermute(views[i - 1], 'gy', [(h, (h - 1) % workers) for h in range(w...]
    all_gather x1 -> x0, waiting for transfers between devices: 106 us -> none  [per_device(): lax.all_gather(down_weight, 'gy', axis=1, tiled=True)]
    all_gather x1, waiting for transfers between devices: 105 us -> 34.6 us  [per_device(): lax.all_gather(up_weight, 'gy', axis=0, tiled=True)]
    psum x2, waiting for transfers between devices: 140 us -> 74 us  [finish_sum(): summed = lax.psum(head_partial, 'gx')]
    ppermute x0 -> x7, starting transfers between devices: none -> 33.6 us  [convert_lots_all(): lax.ppermute(views[i - 1], 'gy', [(h, (h - 1) % workers) for h in range(w...]
    unnamed x9 -> x38, local copies, waits for them, and re-layouts: 5.68 us -> 29.2 us
  transfers between devices with their start and end apart: 8 -> 14, of which waited for: 8 -> 13; matrix products, arithmetic and copies ran while one was open for 5% -> 8% of each run, Pallas kernels for 0% -> 0%
where the time goes in v1:
time: 763 us; the launch traced here: 762 us
  waiting for transfers between devices  533 us (70%)
  blocking collectives  81 us (11%)
  local copies, waits for them, and re-layouts  49.2 us (6%)
  matrix products  40.8 us (5%)
  starting transfers between devices  33.9 us (4%)
  between operations  14.3 us (2%)
  other arithmetic  9.36 us (1%)
    all_gather x1, waiting for transfers between devices, per_device(): lax.all_gather(merge_weight, 'gy', axis=0, tiled=True)  141 us
    ppermute x7, waiting for transfers between devices, convert_lots_all(): lax.ppermute(views[i - 1], 'gy', [(h, (h - 1) % workers) for h in range(w...  131 us
    all_gather x1, waiting for transfers between devices, per_device(): lax.all_gather(qkv_weight, 'gy', axis=0, tiled=True)  104 us
    psum x2, waiting for transfers between devices, finish_sum(): summed = lax.psum(head_partial, 'gx')  74 us
    psum x1, blocking collectives, per_device(): request_sq = lax.psum(request_part, ('gx', 'gy'))  42.4 us
    pmax x1, blocking collectives, per_device(): top_logit = lax.pmax(local_top, ('gx', 'gy'))  38.6 us
    all_gather x1, waiting for transfers between devices, per_device(): lax.all_gather(up_weight, 'gy', axis=0, tiled=True)  34.6 us
    ppermute x7, starting transfers between devices, convert_lots_all(): lax.ppermute(views[i - 1], 'gy', [(h, (h - 1) % workers) for h in range(w...  33.6 us
  transfers between devices with their start and end apart: 14, of which 13 were waited for; matrix products, arithmetic and copies ran while one was open for 8% of the time, Pallas kernels for 0%

profile of v1, /device:TPU:0, one launch (start us, length us, event | category | flops | bytes accessed | tf_op | source)
XLA Modules:
  0.0 762.0 jit_solution(6157236095673628723)
XLA Ops:
  13.4 19.2 %all-gather.6.cloned.1.call-done = bf16[512,1664]{0,1:T(8,128)(2,1)} async-done(((bf16[512,416]{0,1:T(8,128)(2,1)}), bf16[512,1664]{0,1:T(8,128)(2,1)}) %all-gather.6.cloned.1.call-update) | async-done | bytes 1703952 | tf_op jit(solution)/shard_map/all_gather | solution.py:59
  36.1 104.4 %all-gather.8.cloned.1.call-done = bf16[1664,3,416]{2,1,0:T(4,128)(2,1)} async-done(((bf16[208,3,416]{2,1,0:T(4,128)(2,1)}), bf16[1664,3,416]{2,1,0:T(4,128)(2,1)}) %all-gather.8.cloned.1.call-update) | async-done | bytes 4153360 | tf_op jit(solution)/shard_map/all_gather | solution.py:63
  140.5 11.2 %copy.30 = bf16[1664,3,416]{0,2,1:T(8,128)(2,1)} copy(bf16[1664,3,416]{2,1,0:T(4,128)(2,1)} %all-gather.8.cloned.1.call-done) | data formatting | bytes 8306688 | tf_op jit(solution)/shard_map/all_gather | solution.py:63
  159.9 26.8 %all-gather.10.cloned.1.call-done = bf16[416,1664]{0,1:T(8,128)(2,1)} async-done(((bf16[416,208]{0,1:T(8,128)(2,1)}), bf16[416,1664]{0,1:T(8,128)(2,1)}) %all-gather.10.cloned.1.call-update) | async-done | bytes 1384464 | tf_op jit(solution)/shard_map/all_gather | solution.py:75
  194.2 18.1 %collective-permute-done = bf16[2048,208]{0,1:T(8,128)(2,1)S(1)} collective-permute-done((bf16[2048,208]{0,1:T(8,128)(2,1)S(1)}, bf16[2048,208]{0,1:T(8,128)(2,1)S(1)}, u32[]{:S(2)}, u32[]{:S(2)}) %collective-permute-start) | collective-permute-done | bytes 852000 | tf_op jit(solution)/shard_map/ppermute | solution.py:17
  212.3 5.2 collective-permute-start.1
  217.5 17.2 %collective-permute-done.1 = bf16[2048,208]{0,1:T(8,128)(2,1)S(1)} collective-permute-done((bf16[2048,208]{0,1:T(8,128)(2,1)S(1)}, bf16[2048,208]{0,1:T(8,128)(2,1)S(1)}, u32[]{:S(2)}, u32[]{:S(2)}) %collective-permute-start.1) | collective-permute-done | bytes 852000 | tf_op jit(solution)/shard_map/ppermute | solution.py:17
  235.7 5.2 collective-permute-start.2
  240.9 16.3 %collective-permute-done.2 = bf16[2048,208]{0,1:T(8,128)(2,1)S(1)} collective-permute-done((bf16[2048,208]{0,1:T(8,128)(2,1)S(1)}, bf16[2048,208]{0,1:T(8,128)(2,1)S(1)}, u32[]{:S(2)}, u32[]{:S(2)}) %collective-permute-start.2) | collective-permute-done | bytes 852000 | tf_op jit(solution)/shard_map/ppermute | solution.py:17
  258.1 5.2 collective-permute-start.3
  263.3 25.4 %collective-permute-done.3 = bf16[2048,208]{0,1:T(8,128)(2,1)S(1)} collective-permute-done((bf16[2048,208]{0,1:T(8,128)(2,1)S(1)}, bf16[2048,208]{0,1:T(8,128)(2,1)S(1)}, u32[]{:S(2)}, u32[]{:S(2)}) %collective-permute-start.3) | collective-permute-done | bytes 852000 | tf_op jit(solution)/shard_map/ppermute | solution.py:17
  289.6 5.2 collective-permute-start.4
  294.9 31.9 %collective-permute-done.4 = bf16[2048,208]{0,1:T(8,128)(2,1)} collective-permute-done((bf16[2048,208]{0,1:T(8,128)(2,1)S(1)}, bf16[2048,208]{0,1:T(8,128)(2,1)}, u32[]{:S(2)}, u32[]{:S(2)}) %collective-permute-start.4) | collective-permute-done | bytes 852000 | tf_op jit(solution)/shard_map/ppermute | solution.py:17
  326.7 5.3 collective-permute-start.5
  336.2 9.8 %collective-permute-done.5 = bf16[2048,208]{0,1:T(8,128)(2,1)} collective-permute-done((bf16[2048,208]{0,1:T(8,128)(2,1)}, bf16[2048,208]{0,1:T(8,128)(2,1)}, u32[]{:S(2)}, u32[]{:S(2)}) %collective-permute-start.5) | collective-permute-done | bytes 852000 | tf_op jit(solution)/shard_map/ppermute | solution.py:17
  346.0 5.2 collective-permute-start.6
  357.6 12.5 %collective-permute-done.6 = bf16[2048,208]{0,1:T(8,128)(2,1)S(1)} collective-permute-done((bf16[2048,208]{0,1:T(8,128)(2,1)}, bf16[2048,208]{0,1:T(8,128)(2,1)S(1)}, u32[]{:S(2)}, u32[]{:S(2)}) %collective-permute-start.6) | collective-permute-done | bytes 852000 | tf_op jit(solution)/shard_map/ppermute | solution.py:17
  384.0 34.6 %all-gather.12.cloned.1.call-done = bf16[1664,2048]{1,0:T(8,128)(2,1)} async-done(((bf16[208,2048]{1,0:T(8,128)(2,1)}), bf16[1664,2048]{1,0:T(8,128)(2,1)}) %all-gather.12.cloned.1.call-update) | async-done | bytes 6815760 | tf_op jit(solution)/shard_map/all_gather | solution.py:80
  418.6 21.9 %fusion.1 = f32[512,1664]{1,0:T(8,128)} fusion(bf16[2048,3328]{0,1:T(8,128)(2,1)} %constant_dynamic-update-slice_fusion, s32[]{:T(128)S(6)} %select_n.56, bf16[1664,2048]{1,0:T(8,128)(2,1)} %all-gather.12.cloned.1.call-done, bf16[512,1664]{1,0:T(8,128)(2,1)S(1)} %get-tuple-element.7, f32[512]{0:T(512)S(1)} %get-tuple-element.13, f32[512]{0:T(512)S(1)} %get-tuple-element.12), kind=kOutput, calls=%fused_computation.2 | convolution fusion | flops 7050887168 | bytes 18747396 | tf_op jit(solution)/shard_map/dot_general | solution.py:82
  441.8 74.0 %all-reduce.5.cloned.1.call-done = f32[512,1664]{1,0:T(8,128)} async-done(((f32[512,1664]{1,0:T(8,128)}), f32[512,1664]{1,0:T(8,128)}) %all-reduce.5.cloned.1.call-update) | async-done | bytes 3407888 | tf_op jit(solution)/shard_map/psum | solution.py:39
  520.5 42.4 %psum.23 = f32[8]{0:T(128)S(1)} all-reduce(f32[8]{0:T(128)S(1)} %select_reduce_fusion.1), channel_id=1, replica_groups=mesh['gx'=4,'gy'=8] {'gx','gy'}, use_global_device_ids=true, to_apply=%region_11.12 | all-reduce | flops 8 | bytes 64 | tf_op jit(solution)/shard_map/psum | solution.py:100
  567.0 141.2 %all-gather.14.cloned.1.call-done = bf16[6656,1024]{1,0:T(8,128)(2,1)} async-done(((bf16[832,1024]{1,0:T(8,128)(2,1)}), bf16[6656,1024]{1,0:T(8,128)(2,1)}) %all-gather.14.cloned.1.call-update) | async-done | bytes 13631504 | tf_op jit(solution)/shard_map/all_gather | solution.py:98
  708.2 8.4 %fusion.110 = (f32[]{:T(128)}, bf16[128,1024]{1,0:T(8,128)(2,1)}) fusion(bf16[6656,1024]{1,0:T(8,128)(2,1)} %all-gather.14.cloned.1.call-done, pred[128,6656]{1,0:T(8,128)(4,1)} %bitcast.25, bf16[128,6656]{1,0:T(8,128)(2,1)S(1)} %gather.7), kind=kOutput, calls=%fused_computation.156 | convolution fusion | flops 1745944576 | bytes 16449540 | tf_op jit(solution)/shard_map/dot_general | solution.py:34
  716.6 38.6 %pmax.7 = f32[]{:T(128)} all-reduce(f32[]{:T(128)} %get-tuple-element.10), channel_id=1, replica_groups=mesh['gx'=4,'gy'=8] {'gx','gy'}, use_global_device_ids=true, to_apply=%region_13.14 | all-reduce | flops 1 | bytes 8 | tf_op jit(solution)/shard_map/pmax | solution.py:101
  (82 shorter events, 62.4 us)
Async XLA Ops:
  7.2 25.5 %all-gather.6.cloned.1.call-start = ((), (), s32[]{:S(2)}) async-start(), calls=%async_computation | async-start | bytes 2129920 | tf_op jit(solution)/shard_map/all_gather | solution.py:59
  7.9 132.6 %all-gather.8.cloned.1.call-start = ((), (), s32[]{:S(2)}) async-start(), calls=%async_computation.1 | async-start | bytes 7667712 | tf_op jit(solution)/shard_map/all_gather | solution.py:63
  10.6 176.1 %all-gather.10.cloned.1.call-start = ((), (), s32[]{:S(2)}) async-start(), calls=%async_computation.2 | async-start | bytes 1916928 | tf_op jit(solution)/shard_map/all_gather | solution.py:75
  12.4 368.9 %all-reduce.3.cloned.1.call-start = ((), (), s32[]{:S(2)}) async-start(), calls=%async_computation.3 | async-start | bytes 6815744 | tf_op jit(solution)/shard_map/psum | solution.py:39
  186.7 5.2 copy-start
  191.2 227.4 %all-gather.12.cloned.1.call-start = ((), (), s32[]{:S(2)}) async-start(), calls=%async_computation.4 | async-start | bytes 7667712 | tf_op jit(solution)/shard_map/all_gather | solution.py:80
  191.8 323.9 %all-reduce.5.cloned.1.call-start = ((), (), s32[]{:S(2)}) async-start(), calls=%async_computation.5 | async-start | bytes 6815744 | tf_op jit(solution)/shard_map/psum | solution.py:39
  191.9 20.4 %collective-permute-start = (bf16[2048,208]{0,1:T(8,128)(2,1)S(1)}, bf16[2048,208]{0,1:T(8,128)(2,1)S(1)}, u32[]{:S(2)}, u32[]{:S(2)}) collective-permute-start(bf16[2048,208]{0,1:T(8,128)(2,1)S(1)} %copy-done), channel_id=1, source_target_pairs={{0,7},{1,0},{2,1},{3,2},{4,3},{5,4},{6,5},{7,6},{8,15},{9,8},{10,9... | collective-permute-start | bytes 2555912 | tf_op jit(solution)/shard_map/ppermute | solution.py:17
  212.3 22.4 %collective-permute-start.1 = (bf16[2048,208]{0,1:T(8,128)(2,1)S(1)}, bf16[2048,208]{0,1:T(8,128)(2,1)S(1)}, u32[]{:S(2)}, u32[]{:S(2)}) collective-permute-start(bf16[2048,208]{0,1:T(8,128)(2,1)S(1)} %collective-permute-done), channel_id=1, source_target_pairs={{0,7},{1,0},{2,1},{3,2},{4,3},{5,4},{6,5},{7,6},{8,15},{9,8},{10,9... | collective-permute-start | bytes 2555912 | tf_op jit(solution)/shard_map/ppermute | solution.py:17
  234.7 0.9 copy-start.1
  235.7 21.5 %collective-permute-start.2 = (bf16[2048,208]{0,1:T(8,128)(2,1)S(1)}, bf16[2048,208]{0,1:T(8,128)(2,1)S(1)}, u32[]{:S(2)}, u32[]{:S(2)}) collective-permute-start(bf16[2048,208]{0,1:T(8,128)(2,1)S(1)} %collective-permute-done.1), channel_id=1, source_target_pairs={{0,7},{1,0},{2,1},{3,2},{4,3},{5,4},{6,5},{7,6},{8,15},{9,8},{10,9... | collective-permute-start | bytes 2555912 | tf_op jit(solution)/shard_map/ppermute | solution.py:17
  257.2 0.9 copy-start.3
  258.1 30.6 %collective-permute-start.3 = (bf16[2048,208]{0,1:T(8,128)(2,1)S(1)}, bf16[2048,208]{0,1:T(8,128)(2,1)S(1)}, u32[]{:S(2)}, u32[]{:S(2)}) collective-permute-start(bf16[2048,208]{0,1:T(8,128)(2,1)S(1)} %collective-permute-done.2), channel_id=1, source_target_pairs={{0,7},{1,0},{2,1},{3,2},{4,3},{5,4},{6,5},{7,6},{8,15},{9,8},{10,9... | collective-permute-start | bytes 2555912 | tf_op jit(solution)/shard_map/ppermute | solution.py:17
  288.7 0.9 copy-start.5
  289.6 37.1 %collective-permute-start.4 = (bf16[2048,208]{0,1:T(8,128)(2,1)S(1)}, bf16[2048,208]{0,1:T(8,128)(2,1)}, u32[]{:S(2)}, u32[]{:S(2)}) collective-permute-start(bf16[2048,208]{0,1:T(8,128)(2,1)S(1)} %collective-permute-done.3), channel_id=1, source_target_pairs={{0,7},{1,0},{2,1},{3,2},{4,3},{5,4},{6,5},{7,6},{8,15},{9,8},{10,9... | collective-permute-start | bytes 2555912 | tf_op jit(solution)/shard_map/ppermute | solution.py:17
  326.7 19.3 %collective-permute-start.5 = (bf16[2048,208]{0,1:T(8,128)(2,1)}, bf16[2048,208]{0,1:T(8,128)(2,1)}, u32[]{:S(2)}, u32[]{:S(2)}) collective-permute-start(bf16[2048,208]{0,1:T(8,128)(2,1)} %collective-permute-done.4), channel_id=1, source_target_pairs={{0,7},{1,0},{2,1},{3,2},{4,3},{5,4},{6,5},{7,6},{8,15},{9,8},{10,9... | collective-permute-start | bytes 2555912 | tf_op jit(solution)/shard_map/ppermute | solution.py:17
  332.1 19.2 %copy-start.4 = (bf16[2048,208]{0,1:T(8,128)(2,1)S(1)}, bf16[2048,208]{0,1:T(8,128)(2,1)}, u32[]{:S(2)}) copy-start(bf16[2048,208]{0,1:T(8,128)(2,1)} %copy-done.3) | copy-start | bytes 2555908
  332.1 20.1 %copy-start.6 = (bf16[2048,208]{0,1:T(8,128)(2,1)S(1)}, bf16[2048,208]{0,1:T(8,128)(2,1)}, u32[]{:S(2)}) copy-start(bf16[2048,208]{0,1:T(8,128)(2,1)} %copy-done.5) | copy-start | bytes 2555908
  346.0 24.0 %collective-permute-start.6 = (bf16[2048,208]{0,1:T(8,128)(2,1)}, bf16[2048,208]{0,1:T(8,128)(2,1)S(1)}, u32[]{:S(2)}, u32[]{:S(2)}) collective-permute-start(bf16[2048,208]{0,1:T(8,128)(2,1)} %collective-permute-done.5), channel_id=1, source_target_pairs={{0,7},{1,0},{2,1},{3,2},{4,3},{5,4},{6,5},{7,6},{8,15},{9,8},{10,9... | collective-permute-start | bytes 2555912 | tf_op jit(solution)/shard_map/ppermute | solution.py:17
  353.2 19.8 %copy-start.2 = (bf16[2048,208]{0,1:T(8,128)(2,1)S(1)}, bf16[2048,208]{0,1:T(8,128)(2,1)}, u32[]{:S(2)}) copy-start(bf16[2048,208]{0,1:T(8,128)(2,1)} %copy-done.1) | copy-start | bytes 2555908
  440.5 0.8 copy-start.8
  440.5 1.2 copy-start.9
  440.5 267.7 %all-gather.14.cloned.1.call-start = ((), (), s32[]{:S(2)}) async-start(), calls=%async_computation.6 | async-start | bytes 15335424 | tf_op jit(solution)/shard_map/all_gather | solution.py:98
  441.3 77.1 %copy-start.7 = (s32[512]{0:T(512)S(1)}, s32[512]{0:T(512)}, u32[]{:S(2)}) copy-start(s32[512]{0:T(512)} %param.10) | copy-start | bytes 6148
Sparse Core Ops, SparseCore 0:
  9.6 23.0 all-gather.5
  34.9 105.5 all-gather.7
  143.2 43.4 all-gather.9
  191.4 71.6 all-reduce.2
  265.1 153.5 all-gather.11
  440.6 75.0 all-reduce.4
  517.9 190.2 all-gather.13
